TPU v7x, 256 devices: a whole 4x4x8 slice. The times are simulated.
256 devices in a mesh: dp: 2 (over y_hi), fsdp: 16 (over x, y_lo, core), tensor: 8 (over z).
Axes of the slice: x: 4, y: 4 (y_hi: 2, y_lo: 2; y = y_hi * 2 + y_lo), z: 8, core: 2. Of those that a mesh axis runs over, the one named last changes fastest.
Arguments:
- activations: bfloat16 [4096, 8192], P(('dp', 'fsdp'), 'tensor'), may hold values from -6 to 6
- cotangent: bfloat16 [4096, 8192], P(('dp', 'fsdp'), 'tensor'), may hold values from -6 to 6
- up_tiles: bfloat16 [1024, 128, 128], P(('fsdp', 'tensor')), may hold values from -0.1875 to 0.1875
- down_tiles: bfloat16 [1024, 128, 128], P(('fsdp', 'tensor')), may hold values from -0.125 to 0.125
- up_rows: int32 [128, 8], P(None, 'tensor'), may hold values from 0 to 63, as said below
- up_cols: int32 [128, 8], P(None, 'tensor'), may hold values from 0 to 15, as said below
- down_rows: int32 [128, 8], P(None, 'tensor'), may hold values from 0 to 15, as said below
- down_cols: int32 [128, 8], P(None, 'tensor'), may hold values from 0 to 63, as said below
Outputs:
- output: bfloat16 [4096, 8192], P(('dp', 'fsdp'), 'tensor')
- input_grad: bfloat16 [4096, 8192], P(('dp', 'fsdp'), 'tensor')
- up_grad: float32 [1024, 128, 128], P(('fsdp', 'tensor'))
- down_grad: float32 [1024, 128, 128], P(('fsdp', 'tensor'))
Inputs may be any that keep to these rules, and one draw needn't show every extreme that they name: `up_rows`: within a column, the up tiles of one hidden-unit block name distinct feature blocks. `up_cols`: every value occurs exactly 8 times in each column. `down_rows`: every value occurs exactly 8 times in each column. `down_cols`: within a column, the down tiles of one hidden-unit block name distinct feature blocks.
All inputs are finite; a program needn't handle non-finite values.
Results may differ from a plain program's by a relative error of at most 0.018.
Values may be sent and summed in bfloat16 or wider, within the bound.
No kernel may reach another device: no remote copies, remote signals or barrier semaphores. Data moves between devices by JAX's collectives and lax.ppermute only.
A program may use at most 128 MiB of HBM per device.

v0:
```python
import jax
import jax.numpy as jnp
from jax import lax
from jax.sharding import PartitionSpec as P

D = 8192
FF = 16384
inv_root_two = 0.7071067811865476
inv_root_tau = 0.3989422804014327


def gelu_parts(values):
    normal_cdf = 0.5 * (1.0 + jax.scipy.special.erf(values * inv_root_two))
    density = inv_root_tau * jnp.exp(-0.5 * values * values)
    return (values * normal_cdf, normal_cdf + values * density)


def grouped_pick(acting, far_index, hidden_blocks, block_size):
    rows_here = acting.shape[0]
    picked = acting.reshape(rows_here, -1, block_size)[:, far_index]
    return picked.reshape(rows_here, hidden_blocks, -1, block_size)


def add_far(product, far_index, model_blocks):
    rows_here = product.shape[0]
    block_size = product.shape[-1]
    flat = product.reshape(rows_here, -1, block_size)
    summed = (
        jnp.zeros((rows_here, model_blocks, block_size), jnp.float32).at[:, far_index].add(flat)
    )
    return summed.reshape(rows_here, model_blocks * block_size)


def grouped_tiles(tiles, order, hidden_blocks):
    block_size = tiles.shape[1]
    return tiles[order].reshape(hidden_blocks, -1, block_size, block_size)


def body(activations, cotangent, up_tiles, down_tiles, up_rows, up_cols, down_rows, down_cols):
    block_size = up_tiles.shape[1]
    hidden_blocks = FF // (block_size * lax.axis_size("tensor"))
    model_blocks = D // block_size
    up_order = jnp.argsort(up_cols[:, 0], stable=True)
    down_order = jnp.argsort(down_rows[:, 0], stable=True)
    up_back = jnp.argsort(up_order)
    down_back = jnp.argsort(down_order)
    up_far = up_rows[:, 0][up_order]
    down_far = down_cols[:, 0][down_order]
    full_input = lax.all_gather(activations, "tensor", axis=1, tiled=True)
    input_pick = grouped_pick(full_input, up_far, hidden_blocks, block_size)
    up_whole = lax.all_gather(up_tiles, "fsdp", axis=0, tiled=True)
    up_sorted = grouped_tiles(up_whole, up_order, hidden_blocks)
    pre_act = jnp.einsum(
        "thkb,hkbc->thc", input_pick, up_sorted, preferred_element_type=jnp.float32
    )
    gelu_out, gelu_slope = gelu_parts(pre_act)
    hidden = gelu_out.astype(jnp.bfloat16)
    down_whole = lax.all_gather(down_tiles, "fsdp", axis=0, tiled=True)
    down_sorted = grouped_tiles(down_whole, down_order, hidden_blocks)
    out_product = jnp.einsum(
        "thb,hkbc->thkc", hidden, down_sorted, preferred_element_type=jnp.float32
    )
    partial_out = add_far(out_product, down_far, model_blocks)
    output = lax.psum_scatter(
        partial_out.astype(jnp.bfloat16), "tensor", scatter_dimension=1, tiled=True
    )
    full_cotangent = lax.all_gather(cotangent, "tensor", axis=1, tiled=True)
    cot_pick = grouped_pick(full_cotangent, down_far, hidden_blocks, block_size)
    hidden_grad = jnp.einsum(
        "thkc,hkbc->thb", cot_pick, down_sorted, preferred_element_type=jnp.float32
    )
    pre_grad = (hidden_grad * gelu_slope).astype(jnp.bfloat16)
    in_product = jnp.einsum(
        "thc,hkbc->thkb", pre_grad, up_sorted, preferred_element_type=jnp.float32
    )
    partial_in = add_far(in_product, up_far, model_blocks)
    input_grad = lax.psum_scatter(
        partial_in.astype(jnp.bfloat16), "tensor", scatter_dimension=1, tiled=True
    )
    up_grouped = jnp.einsum(
        "thkb,thc->hkbc", input_pick, pre_grad, preferred_element_type=jnp.float32
    )
    down_grouped = jnp.einsum(
        "thb,thkc->hkbc", hidden, cot_pick, preferred_element_type=jnp.float32
    )
    up_rounded = up_grouped.astype(jnp.bfloat16).reshape(-1, block_size, block_size)
    down_rounded = down_grouped.astype(jnp.bfloat16).reshape(-1, block_size, block_size)
    up_term = up_rounded[up_back].astype(jnp.float32)
    down_term = down_rounded[down_back].astype(jnp.float32)
    up_part, down_part = (
        lax.psum_scatter(
            up_term.astype(jnp.bfloat16), "fsdp", scatter_dimension=0, tiled=True
        ).astype(jnp.float32),
        lax.psum_scatter(
            down_term.astype(jnp.bfloat16), "fsdp", scatter_dimension=0, tiled=True
        ).astype(jnp.float32),
    )
    up_grad, down_grad = (
        lax.psum(up_part.astype(jnp.bfloat16), "dp").astype(jnp.float32),
        lax.psum(down_part.astype(jnp.bfloat16), "dp").astype(jnp.float32),
    )
    return (output, input_grad, up_grad, down_grad)


def solution(mesh):
    in_specs = (
        P(("dp", "fsdp"), "tensor"),
        P(("dp", "fsdp"), "tensor"),
        P(("fsdp", "tensor"), None, None),
        P(("fsdp", "tensor"), None, None),
        P(None, "tensor"),
        P(None, "tensor"),
        P(None, "tensor"),
        P(None, "tensor"),
    )
    out_specs = (
        P(("dp", "fsdp"), "tensor"),
        P(("dp", "fsdp"), "tensor"),
        P(("fsdp", "tensor"), None, None),
        P(("fsdp", "tensor"), None, None),
    )
    return jax.shard_map(body, mesh=mesh, in_specs=in_specs, out_specs=out_specs, check_vma=False)
```

profile of v0, /device:TPU:1, one launch (start us, length us, event | category | flops | bytes accessed | tf_op | source)
XLA Modules:
  0.0 480.6 jit_solution(9236470539080875752)
XLA Ops:
  24.1 28.0 %all-gather.9.cloned.1.call-done = bf16[128,8192]{0,1:T(8,128)(2,1)} async-done(((bf16[128,1024]{0,1:T(8,128)(2,1)}), bf16[128,8192]{0,1:T(8,128)(2,1)}) %all-gather.9.cloned.1.call-update) | async-done | bytes 2097168 | tf_op jit(solution)/shard_map/all_gather | solution.py:49
  55.3 39.0 %all-gather.11.cloned.1.call-done = bf16[128,8192]{0,1:T(8,128)(2,1)} async-done(((bf16[128,1024]{0,1:T(8,128)(2,1)}), bf16[128,8192]{0,1:T(8,128)(2,1)}) %all-gather.11.cloned.1.call-update) | async-done | bytes 2097168 | tf_op jit(solution)/shard_map/all_gather | solution.py:67
  94.3 4.1 copy.66
  101.4 4.6 gather_fusion.5
  106.0 32.7 %all-gather.7.cloned.1.call-done = bf16[128,128,128]{2,1,0:T(8,128)(2,1)} async-done(((bf16[8,128,128]{2,1,0:T(8,128)(2,1)}), bf16[128,128,128]{2,1,0:T(8,128)(2,1)}) %all-gather.7.cloned.1.call-update) | async-done | bytes 4194320 | tf_op jit(solution)/shard_map/all_gather | solution.py:51
  138.7 5.2 %gather_fusion.2 = bf16[128,128,128]{2,1,0:T(8,128)(2,1)} fusion(bf16[128,128,128]{2,1,0:T(8,128)(2,1)} %all-gather.7.cloned.1.call-done, s32[1024]{0:T(1024)S(1)} %pad_clamp_fusion.4), kind=kCustom, calls=%fused_computation.2 | custom fusion | bytes 8389120 | tf_op jit(solution)/shard_map/gather | solution.py:36
  143.9 4.8 convolution_bitcast_fusion.1
  148.7 31.7 %all-gather.5.cloned.1.call-done = bf16[128,128,128]{2,1,0:T(8,128)(2,1)} async-done(((bf16[8,128,128]{2,1,0:T(8,128)(2,1)}), bf16[128,128,128]{2,1,0:T(8,128)(2,1)}) %all-gather.5.cloned.1.call-update) | async-done | bytes 4194320 | tf_op jit(solution)/shard_map/all_gather | solution.py:58
  180.5 5.2 %gather_fusion.1 = bf16[128,128,128]{2,1,0:T(8,128)(2,1)} fusion(bf16[128,128,128]{2,1,0:T(8,128)(2,1)} %all-gather.5.cloned.1.call-done, s32[1024]{0:T(1024)S(1)} %pad_clamp_fusion.5), kind=kCustom, calls=%fused_computation.1 | custom fusion | bytes 8389120 | tf_op jit(solution)/shard_map/gather | solution.py:36
  185.7 5.0 %fusion.2 = bf16[128,16,128,1]{0,2,3,1:T(8,128)(2,1)S(1)} fusion(bf16[16,8,128,128]{3,2,1,0:T(8,128)(2,1)} %bitcast.84, bf16[128,16,8,128]{3,0,2,1:T(8,128)(2,1)} %bitcast.86, f32[128,16,128]{0,2,1:T(8,128)S(1)} %convolution_bitcast_fusion.1), kind=kOutput, calls=%fused_computation.17 | convolution fusion | flops 539492352 | bytes 9961472 | tf_op jit(solution)/shard_map/thkc,hkbc->thb/dot_general | solution.py:69
  194.0 5.2 %gather_fusion.6 = bf16[128,128,128]{2,1,0:T(8,128)(2,1)} fusion(bf16[128,128,128]{2,1,0:T(8,128)(2,1)} %bitcast.88, s32[1024]{0:T(1024)S(1)} %pad_clamp_fusion.1), kind=kCustom, calls=%fused_computation.6 | custom fusion | bytes 8389120 | tf_op jit(solution)/shard_map/gather | solution.py:88
  202.0 5.6 %convolution_convert_fusion = bf16[16,8,128,128]{3,2,1,0:T(8,128)(2,1)} fusion(bf16[128,16,8,128]{3,0,2,1:T(8,128)(2,1)} %bitcast.87, f32[128,16,128]{0,2,1:T(8,128)S(1)} %convolution_bitcast_fusion.1), kind=kOutput, calls=%fused_computation.10 | convolution fusion | flops 540278784 | bytes 9437184 | tf_op jit(solution)/shard_map/thb,thkc->hkbc/dot_general | solution.py:83
  207.6 6.4 %copy.74 = bf16[128,128,128]{2,1,0:T(8,128)(2,1)} copy(bf16[128,128,128]{1,2,0:T(8,128)(2,1)} %bitcast.89) | data formatting | bytes 8388608 | tf_op jit(solution)/shard_map/reshape | solution.py:87
  214.0 5.3 %gather_fusion.7 = bf16[128,128,128]{2,1,0:T(8,128)(2,1)} fusion(bf16[128,128,128]{2,1,0:T(8,128)(2,1)} %copy.74, s32[1024]{0:T(1024)S(1)} %pad_clamp_fusion), kind=kCustom, calls=%fused_computation.7 | custom fusion | bytes 8389120 | tf_op jit(solution)/shard_map/gather | solution.py:89
  219.4 6.7 %fusion.13 = f32[16,8,128,128]{3,2,1,0:T(8,128)} fusion(bf16[16,8,128,128]{3,2,1,0:T(8,128)(2,1)} %bitcast.77, bf16[128,16,128,1]{0,2,3,1:T(8,128)(2,1)S(1)} %fusion.2), kind=kOutput, calls=%fused_computation.40 | convolution fusion | flops 536870912 | bytes 13107200 | tf_op jit(solution)/shard_map/thc,hkbc->thkb/dot_general | solution.py:73
  226.1 9.0 %copy.68 = f32[128,128,128]{2,0,1:T(8,128)} copy(f32[128,128,128]{0,2,1:T(8,128)} %bitcast.82) | data formatting | bytes 16777216 | tf_op jit(solution)/shard_map/reshape | solution.py:27
  237.6 26.7 %scatter_fusion.1 = f32[128,64,128]{2,0,1:T(8,128)} fusion(f32[128,64,128]{2,0,1:T(8,128)} %broadcast.42.clone.1, s32[128]{0:T(128)S(1)} %fusion.9, f32[128,128,128]{2,1,0:T(8,128)} %bitcast.81), kind=kCustom, calls=%fused_computation.9 | custom fusion | flops 2097152 | bytes 25166336 | tf_op jit(solution)/shard_map/scatter-add | solution.py:29
  270.0 6.8 %fusion.11 = f32[16,8,128,128]{3,2,1,0:T(8,128)} fusion(bf16[16,8,128,128]{3,2,1,0:T(8,128)(2,1)} %bitcast.85, f32[128,16,128]{0,2,1:T(8,128)S(1)} %convolution_bitcast_fusion.1), kind=kOutput, calls=%fused_computation.39 | convolution fusion | flops 538181632 | bytes 13631488 | tf_op jit(solution)/shard_map/thb,hkbc->thkc/dot_general | solution.py:60
  276.7 9.0 %copy.63 = f32[128,128,128]{2,0,1:T(8,128)} copy(f32[128,128,128]{0,2,1:T(8,128)} %bitcast.83) | data formatting | bytes 16777216 | tf_op jit(solution)/shard_map/reshape | solution.py:27
  288.2 26.9 %scatter_fusion = f32[128,64,128]{2,0,1:T(8,128)} fusion(f32[128,64,128]{2,0,1:T(8,128)} %broadcast.42.clone, s32[128]{0:T(128)S(1)} %fusion.8, f32[128,128,128]{2,1,0:T(8,128)} %bitcast.80), kind=kCustom, calls=%fused_computation.8 | custom fusion | flops 2097152 | bytes 25166336 | tf_op jit(solution)/shard_map/scatter-add | solution.py:29
  320.7 16.4 %reduce-scatter.11.cloned.1.call-done = bf16[8,128,128]{2,1,0:T(8,128)(2,1)} async-done(((bf16[128,128,128]{2,1,0:T(8,128)(2,1)}), bf16[8,128,128]{2,1,0:T(8,128)(2,1)}) %reduce-scatter.11.cloned.1.call-update) | async-done | bytes 262160 | tf_op jit(solution)/shard_map/reduce_scatter | solution.py:94
  337.1 42.2 %reduce-scatter.7.cloned.1.call-done = bf16[128,1024]{0,1:T(8,128)(2,1)} async-done(((bf16[128,8192]{0,1:T(8,128)(2,1)}), bf16[128,1024]{0,1:T(8,128)(2,1)}) %reduce-scatter.7.cloned.1.call-update) | async-done | bytes 262160 | tf_op jit(solution)/shard_map/reduce_scatter | solution.py:77
  381.1 41.9 %reduce-scatter.5.cloned.1.call-done = bf16[128,1024]{0,1:T(8,128)(2,1)} async-done(((bf16[128,8192]{0,1:T(8,128)(2,1)}), bf16[128,1024]{0,1:T(8,128)(2,1)}) %reduce-scatter.5.cloned.1.call-update) | async-done | bytes 262160 | tf_op jit(solution)/shard_map/reduce_scatter | solution.py:64
  424.8 45.7 %all-reduce.3.cloned.1.call-done = (bf16[8,128,128]{2,1,0:T(8,128)(2,1)}, bf16[8,128,128]{2,1,0:T(8,128)(2,1)}) async-done(((bf16[8,128,128]{2,1,0:T(8,128)(2,1)}, bf16[8,128,128]{2,1,0:T(8,128)(2,1)}), (bf16[8,128,128]{2,1,0:T(8,128)(2,1)}, bf16[8,128,128]{2,1,0:T(8,128)(2,1)})) %all-reduce.3.cloned.1.call-update) | async-done | bytes 524304 | tf_op jit(solution)/shard_map/psum | solution.py:99
  (62 shorter events, 52.5 us)
Async XLA Ops:
  7.2 10.9 %copy-start = (s32[128,1]{0,1:T(1,128)S(1)}, s32[128,1]{0,1:T(1,128)}, u32[]{:S(2)}) copy-start(s32[128,1]{0,1:T(1,128)} %param.12) | copy-start | bytes 1540
  7.2 44.9 %all-gather.9.cloned.1.call-start = ((), (), s32[]{:S(2)}) async-start(), calls=%async_computation.6 | async-start | bytes 2359296 | tf_op jit(solution)/shard_map/all_gather | solution.py:49
  9.0 85.3 %all-gather.11.cloned.1.call-start = ((), (), s32[]{:S(2)}) async-start(), calls=%async_computation.8 | async-start | bytes 2359296 | tf_op jit(solution)/shard_map/all_gather | solution.py:67
  10.9 127.8 %all-gather.7.cloned.1.call-start = ((), (), s32[]{:S(2)}) async-start(), calls=%async_computation.5 | async-start | bytes 4456448 | tf_op jit(solution)/shard_map/all_gather | solution.py:51
  11.7 168.8 %all-gather.5.cloned.1.call-start = ((), (), s32[]{:S(2)}) async-start(), calls=%async_computation.4 | async-start | bytes 4456448 | tf_op jit(solution)/shard_map/all_gather | solution.py:58
  12.2 308.5 %reduce-scatter.9.cloned.1.call-start = ((), (), s32[]{:S(2)}) async-start(), calls=%async_computation.10 | async-start | bytes 4456448 | tf_op jit(solution)/shard_map/reduce_scatter | solution.py:91
  185.7 5.0 %copy-start.2 = (bf16[128,128,128]{2,1,0:T(8,128)(2,1)S(1)}, bf16[128,128,128]{2,1,0:T(8,128)(2,1)}, u32[]{:S(2)}) copy-start(bf16[128,128,128]{2,1,0:T(8,128)(2,1)} %gather_fusion.4) | copy-start | bytes 12582916
  199.2 137.9 %reduce-scatter.11.cloned.1.call-start = ((), (), s32[]{:S(2)}) async-start(), calls=%async_computation.11 | async-start | bytes 4456448 | tf_op jit(solution)/shard_map/reduce_scatter | solution.py:94
  219.4 160.0 %reduce-scatter.7.cloned.1.call-start = ((), (), s32[]{:S(2)}) async-start(), calls=%async_computation.9 | async-start | bytes 2359296 | tf_op jit(solution)/shard_map/reduce_scatter | solution.py:77
  269.9 153.1 %reduce-scatter.5.cloned.1.call-start = ((), (), s32[]{:S(2)}) async-start(), calls=%async_computation.7 | async-start | bytes 2359296 | tf_op jit(solution)/shard_map/reduce_scatter | solution.py:64
  315.1 158.9 %copy-start.1 = (s32[128,1]{0,1:T(1,128)S(1)}, s32[128,1]{0,1:T(1,128)}, u32[]{:S(2)}) copy-start(s32[128,1]{0,1:T(1,128)} %param.12) | copy-start | bytes 1540
  320.7 149.9 %all-reduce.3.cloned.1.call-start = ((), (), s32[]{:S(2)}) async-start(), calls=%async_computation.12 | async-start | bytes 1048576 | tf_op jit(solution)/shard_map/psum | solution.py:99
Sparse Core Ops, SparseCore 0:
  10.4 41.6 all-gather.8
  54.5 39.8 all-gather.10
  96.2 42.5 all-gather.6
  140.4 39.9 all-gather.4
  199.3 66.5 reduce-scatter.8
  268.4 68.6 reduce-scatter.10
  339.7 39.6 reduce-scatter.6
  381.9 41.0 reduce-scatter.4
  425.7 44.8 all-reduce.2
where the time goes:
time: 482 us; the launch traced here: 481 us
  waiting for transfers between devices  279 us (58%)
  local copies, waits for them, and re-layouts  81.1 us (17%)
  other arithmetic  73.8 us (15%)
  matrix products  32.2 us (7%)
  between operations  14 us (3%)
    scatter-add x2, other arithmetic, add_far(): jnp.zeros((rows_here, model_blocks, block_size), jnp.float32)  53.6 us
    psum x1, waiting for transfers between devices, body(): lax.psum(up_part.astype(jnp.bfloat16), 'dp').astype(jnp.float32)  45.7 us
    reduce_scatter x1, waiting for transfers between devices, body(): lax.psum_scatter(partial_in.astype(jnp.bfloat16), 'tensor', scatter_dimen...  42.2 us
    reduce_scatter x1, waiting for transfers between devices, body(): lax.psum_scatter(partial_out.astype(jnp.bfloat16), 'tensor', scatter_dime...  41.9 us
    all_gather x1, waiting for transfers between devices, body(): full_cotangent = lax.all_gather(cotangent, 'tensor', axis=1, tiled=True)  39 us
    all_gather x1, waiting for transfers between devices, body(): up_whole = lax.all_gather(up_tiles, 'fsdp', axis=0, tiled=True)  32.7 us
    all_gather x1, waiting for transfers between devices, body(): down_whole = lax.all_gather(down_tiles, 'fsdp', axis=0, tiled=True)  31.7 us
    all_gather x1, waiting for transfers between devices, body(): full_input = lax.all_gather(activations, 'tensor', axis=1, tiled=True)  28 us
  transfers between devices with their start and end apart: 9, of which 8 were waited for; matrix products, arithmetic and copies ran while one was open for 34% of the time, Pallas kernels for 0%

commit v1 on v0

--- a/solution.py
+++ b/solution.py
@@ -64,7 +64,14 @@
     output = lax.psum_scatter(
         partial_out.astype(jnp.bfloat16), "tensor", scatter_dimension=1, tiled=True
     )
-    full_cotangent = lax.all_gather(cotangent, "tensor", axis=1, tiled=True)
+    ring = [cotangent]
+    for hop in range(7):
+        ring.append(lax.ppermute(ring[-1], "tensor", [(dev, (dev + 1) % 8) for dev in range(8)]))
+    full_cotangent = jnp.roll(
+        jnp.concatenate(ring[::-1], axis=1),
+        (lax.axis_index("tensor") + 1) * ring[0].shape[1],
+        axis=1,
+    )
     cot_pick = grouped_pick(full_cotangent, down_far, hidden_blocks, block_size)
     hidden_grad = jnp.einsum(
         "thkc,hkbc->thb", cot_pick, down_sorted, preferred_element_type=jnp.float32

time: 482 us -> 450 us (0.934)
  waiting for transfers between devices: 279 us -> 244 us
    ppermute x0 -> x7, waiting for transfers between devices: none -> 55.5 us  [body(): lax.ppermute(ring[-1], 'tensor', [(dev, (dev + 1) % 8) for dev in range(8)])]
    all_gather x1 -> x0, waiting for transfers between devices: 39 us -> none  [body(): full_cotangent = lax.all_gather(cotangent, 'tensor', axis=1, tiled=True)]
    all_gather x1, waiting for transfers between devices: 28 us -> 0.01 us  [body(): full_input = lax.all_gather(activations, 'tensor', axis=1, tiled=True)]
    all_gather x1, waiting for transfers between devices: 32.7 us -> 6.58 us  [body(): up_whole = lax.all_gather(up_tiles, 'fsdp', axis=0, tiled=True)]
  transfers between devices with their start and end apart: 9 -> 15, of which waited for: 8 -> 13; matrix products, arithmetic and copies ran while one was open for 34% -> 36% of each run, Pallas kernels for 0% -> 0%
where the time goes in v1:
time: 450 us; the launch traced here: 448 us
  waiting for transfers between devices  244 us (54%)
  local copies, waits for them, and re-layouts  80 us (18%)
  other arithmetic  73.9 us (16%)
  matrix products  32.2 us (7%)
  between operations  14.4 us (3%)
    ppermute x7, waiting for transfers between devices, body(): lax.ppermute(ring[-1], 'tensor', [(dev, (dev + 1) % 8) for dev in range(8)])  55.5 us
    scatter-add x2, other arithmetic, add_far(): jnp.zeros((rows_here, model_blocks, block_size), jnp.float32)  53.6 us
    psum x1, waiting for transfers between devices, body(): lax.psum(up_part.astype(jnp.bfloat16), 'dp').astype(jnp.float32)  45.8 us
    reduce_scatter x1, waiting for transfers between devices, body(): lax.psum_scatter(partial_in.astype(jnp.bfloat16), 'tensor', scatter_dimen...  41.9 us
    reduce_scatter x1, waiting for transfers between devices, body(): lax.psum_scatter(partial_out.astype(jnp.bfloat16), 'tensor', scatter_dime...  41.9 us
    all_gather x1, waiting for transfers between devices, body(): down_whole = lax.all_gather(down_tiles, 'fsdp', axis=0, tiled=True)  31.9 us
    reduce_scatter x1, waiting for transfers between devices, body(): lax.psum_scatter(down_term.astype(jnp.bfloat16), 'fsdp', scatter_dimensio...  18.9 us
    reshape x2, local copies, waits for them, and re-layouts, add_far(): flat = product.reshape(rows_here, -1, block_size)  18 us
  transfers between devices with their start and end apart: 15, of which 13 were waited for; matrix products, arithmetic and copies ran while one was open for 36% of the time, Pallas kernels for 0%

profile of v1, /device:TPU:1, one launch (start us, length us, event | category | flops | bytes accessed | tf_op | source)
XLA Modules:
  0.0 448.1 jit_solution(10460431761399955219)
XLA Ops:
  14.2 10.0 %collective-permute-done = bf16[128,1024]{0,1:T(8,128)(2,1)S(1)} collective-permute-done((bf16[128,1024]{0,1:T(8,128)(2,1)S(1)}, bf16[128,1024]{0,1:T(8,128)(2,1)S(1)}, u32[]{:S(2)}, u32[]{:S(2)}) %collective-permute-start) | collective-permute-done | bytes 262176 | tf_op jit(solution)/shard_map/ppermute | solution.py:69
  27.4 6.6 %collective-permute-done.1 = bf16[128,1024]{0,1:T(8,128)(2,1)S(1)} collective-permute-done((bf16[128,1024]{0,1:T(8,128)(2,1)S(1)}, bf16[128,1024]{0,1:T(8,128)(2,1)S(1)}, u32[]{:S(2)}, u32[]{:S(2)}) %collective-permute-start.1) | collective-permute-done | bytes 262176 | tf_op jit(solution)/shard_map/ppermute | solution.py:69
  35.8 11.1 %collective-permute-done.2 = bf16[128,1024]{0,1:T(8,128)(2,1)S(1)} collective-permute-done((bf16[128,1024]{0,1:T(8,128)(2,1)S(1)}, bf16[128,1024]{0,1:T(8,128)(2,1)S(1)}, u32[]{:S(2)}, u32[]{:S(2)}) %collective-permute-start.2) | collective-permute-done | bytes 262176 | tf_op jit(solution)/shard_map/ppermute | solution.py:69
  50.2 10.0 %collective-permute-done.3 = bf16[128,1024]{0,1:T(8,128)(2,1)S(1)} collective-permute-done((bf16[128,1024]{0,1:T(8,128)(2,1)S(1)}, bf16[128,1024]{0,1:T(8,128)(2,1)S(1)}, u32[]{:S(2)}, u32[]{:S(2)}) %collective-permute-start.3) | collective-permute-done | bytes 262176 | tf_op jit(solution)/shard_map/ppermute | solution.py:69
  69.7 5.5 %collective-permute-done.5 = bf16[128,1024]{0,1:T(8,128)(2,1)S(1)} collective-permute-done((bf16[128,1024]{0,1:T(8,128)(2,1)S(1)}, bf16[128,1024]{0,1:T(8,128)(2,1)S(1)}, u32[]{:S(2)}, u32[]{:S(2)}) %collective-permute-start.5) | collective-permute-done | bytes 262176 | tf_op jit(solution)/shard_map/ppermute | solution.py:69
  75.3 9.4 %collective-permute-done.6 = bf16[128,1024]{0,1:T(8,128)(2,1)S(1)} collective-permute-done((bf16[128,1024]{0,1:T(8,128)(2,1)S(1)}, bf16[128,1024]{0,1:T(8,128)(2,1)S(1)}, u32[]{:S(2)}, u32[]{:S(2)}) %collective-permute-start.6) | collective-permute-done | bytes 262176 | tf_op jit(solution)/shard_map/ppermute | solution.py:69
  99.4 6.6 %all-gather.6.cloned.1.call-done = bf16[128,128,128]{2,1,0:T(8,128)(2,1)} async-done(((bf16[8,128,128]{2,1,0:T(8,128)(2,1)}), bf16[128,128,128]{2,1,0:T(8,128)(2,1)}) %all-gather.6.cloned.1.call-update) | async-done | bytes 4194320 | tf_op jit(solution)/shard_map/all_gather | solution.py:51
  106.0 5.2 %gather_fusion.2 = bf16[128,128,128]{2,1,0:T(8,128)(2,1)} fusion(bf16[128,128,128]{2,1,0:T(8,128)(2,1)} %all-gather.6.cloned.1.call-done, s32[1024]{0:T(1024)S(1)} %pad_clamp_fusion.4), kind=kCustom, calls=%fused_computation.2 | custom fusion | bytes 8389120 | tf_op jit(solution)/shard_map/gather | solution.py:36
  116.0 31.9 %all-gather.4.cloned.1.call-done = bf16[128,128,128]{2,1,0:T(8,128)(2,1)} async-done(((bf16[8,128,128]{2,1,0:T(8,128)(2,1)}), bf16[128,128,128]{2,1,0:T(8,128)(2,1)}) %all-gather.4.cloned.1.call-update) | async-done | bytes 4194320 | tf_op jit(solution)/shard_map/all_gather | solution.py:58
  147.8 5.2 %gather_fusion.1 = bf16[128,128,128]{2,1,0:T(8,128)(2,1)} fusion(bf16[128,128,128]{2,1,0:T(8,128)(2,1)} %all-gather.4.cloned.1.call-done, s32[1024]{0:T(1024)S(1)} %pad_clamp_fusion.5), kind=kCustom, calls=%fused_computation.1 | custom fusion | bytes 8389120 | tf_op jit(solution)/shard_map/gather | solution.py:36
  161.4 5.2 %gather_fusion.6 = bf16[128,128,128]{2,1,0:T(8,128)(2,1)} fusion(bf16[128,128,128]{2,1,0:T(8,128)(2,1)} %bitcast.88, s32[1024]{0:T(1024)S(1)} %get-tuple-element.27), kind=kCustom, calls=%fused_computation.6 | custom fusion | bytes 8389120 | tf_op jit(solution)/shard_map/gather | solution.py:95
  166.7 5.6 %convolution_convert_fusion = bf16[16,8,128,128]{3,2,1,0:T(8,128)(2,1)} fusion(bf16[128,16,8,128]{3,0,2,1:T(8,128)(2,1)} %bitcast.87, f32[128,16,128]{0,2,1:T(8,128)S(1)} %convolution_bitcast_fusion.1), kind=kOutput, calls=%fused_computation.10 | convolution fusion | flops 540278784 | bytes 9437184 | tf_op jit(solution)/shard_map/thb,thkc->hkbc/dot_general | solution.py:90
  172.3 6.4 %copy.77 = bf16[128,128,128]{2,1,0:T(8,128)(2,1)} copy(bf16[128,128,128]{1,2,0:T(8,128)(2,1)} %bitcast.89) | data formatting | bytes 8388608 | tf_op jit(solution)/shard_map/reshape | solution.py:94
  178.7 5.2 %gather_fusion.7 = bf16[128,128,128]{2,1,0:T(8,128)(2,1)} fusion(bf16[128,128,128]{2,1,0:T(8,128)(2,1)} %copy.77, s32[1024]{0:T(1024)S(1)} %get-tuple-element.26), kind=kCustom, calls=%fused_computation.7 | custom fusion | bytes 8389120 | tf_op jit(solution)/shard_map/gather | solution.py:96
  184.2 6.7 %fusion.13 = f32[16,8,128,128]{3,2,1,0:T(8,128)} fusion(bf16[16,8,128,128]{3,2,1,0:T(8,128)(2,1)} %bitcast.77, bf16[128,16,128,1]{0,2,3,1:T(8,128)(2,1)S(1)} %fusion.2), kind=kOutput, calls=%fused_computation.57 | convolution fusion | flops 536870912 | bytes 13107200 | tf_op jit(solution)/shard_map/thc,hkbc->thkb/dot_general | solution.py:80
  190.9 9.0 %copy.71 = f32[128,128,128]{2,0,1:T(8,128)} copy(f32[128,128,128]{0,2,1:T(8,128)} %bitcast.82) | data formatting | bytes 16777216 | tf_op jit(solution)/shard_map/reshape | solution.py:27
  202.4 26.7 %scatter_fusion.1 = f32[128,64,128]{2,0,1:T(8,128)} fusion(f32[128,64,128]{2,0,1:T(8,128)} %broadcast.43.clone.1, s32[128]{0:T(128)S(1)} %fusion.9, f32[128,128,128]{2,1,0:T(8,128)} %bitcast.81), kind=kCustom, calls=%fused_computation.9 | custom fusion | flops 2097152 | bytes 25166336 | tf_op jit(solution)/shard_map/scatter-add | solution.py:29
  234.7 6.8 %fusion.11 = f32[16,8,128,128]{3,2,1,0:T(8,128)} fusion(bf16[16,8,128,128]{3,2,1,0:T(8,128)(2,1)} %bitcast.85, f32[128,16,128]{0,2,1:T(8,128)S(1)} %convolution_bitcast_fusion.1), kind=kOutput, calls=%fused_computation.56 | convolution fusion | flops 538181632 | bytes 13631488 | tf_op jit(solution)/shard_map/thb,hkbc->thkc/dot_general | solution.py:60
  241.5 9.0 %copy.64 = f32[128,128,128]{2,0,1:T(8,128)} copy(f32[128,128,128]{0,2,1:T(8,128)} %bitcast.83) | data formatting | bytes 16777216 | tf_op jit(solution)/shard_map/reshape | solution.py:27
  253.0 26.9 %scatter_fusion = f32[128,64,128]{2,0,1:T(8,128)} fusion(f32[128,64,128]{2,0,1:T(8,128)} %broadcast.43.clone, s32[128]{0:T(128)S(1)} %fusion.8, f32[128,128,128]{2,1,0:T(8,128)} %bitcast.80), kind=kCustom, calls=%fused_computation.8 | custom fusion | flops 2097152 | bytes 25166336 | tf_op jit(solution)/shard_map/scatter-add | solution.py:29
  285.6 18.9 %reduce-scatter.11.cloned.1.call-done = bf16[8,128,128]{2,1,0:T(8,128)(2,1)} async-done(((bf16[128,128,128]{2,1,0:T(8,128)(2,1)}), bf16[8,128,128]{2,1,0:T(8,128)(2,1)}) %reduce-scatter.11.cloned.1.call-update) | async-done | bytes 262160 | tf_op jit(solution)/shard_map/reduce_scatter | solution.py:101
  304.5 41.9 %reduce-scatter.7.cloned.1.call-done = bf16[128,1024]{0,1:T(8,128)(2,1)} async-done(((bf16[128,8192]{0,1:T(8,128)(2,1)}), bf16[128,1024]{0,1:T(8,128)(2,1)}) %reduce-scatter.7.cloned.1.call-update) | async-done | bytes 262160 | tf_op jit(solution)/shard_map/reduce_scatter | solution.py:84
  348.2 41.9 %reduce-scatter.5.cloned.1.call-done = bf16[128,1024]{0,1:T(8,128)(2,1)} async-done(((bf16[128,8192]{0,1:T(8,128)(2,1)}), bf16[128,1024]{0,1:T(8,128)(2,1)}) %reduce-scatter.5.cloned.1.call-update) | async-done | bytes 262160 | tf_op jit(solution)/shard_map/reduce_scatter | solution.py:64
  391.9 45.8 %all-reduce.3.cloned.1.call-done = (bf16[8,128,128]{2,1,0:T(8,128)(2,1)}, bf16[8,128,128]{2,1,0:T(8,128)(2,1)}) async-done(((bf16[8,128,128]{2,1,0:T(8,128)(2,1)}, bf16[8,128,128]{2,1,0:T(8,128)(2,1)}), (bf16[8,128,128]{2,1,0:T(8,128)(2,1)}, bf16[8,128,128]{2,1,0:T(8,128)(2,1)})) %all-reduce.3.cloned.1.call-update) | async-done | bytes 524304 | tf_op jit(solution)/shard_map/psum | solution.py:106
  (89 shorter events, 76.1 us)
Async XLA Ops:
  7.2 27.4 %copy-start = (s32[128,1]{0,1:T(1,128)S(1)}, s32[128,1]{0,1:T(1,128)}, u32[]{:S(2)}) copy-start(s32[128,1]{0,1:T(1,128)} %param.15) | copy-start | bytes 1540
  7.2 85.9 %all-gather.8.cloned.1.call-start = ((), (), s32[]{:S(2)}) async-start(), calls=%async_computation.6 | async-start | bytes 2359296 | tf_op jit(solution)/shard_map/all_gather | solution.py:49
  9.0 96.9 %all-gather.6.cloned.1.call-start = ((), (), s32[]{:S(2)}) async-start(), calls=%async_computation.5 | async-start | bytes 4456448 | tf_op jit(solution)/shard_map/all_gather | solution.py:51
  9.8 138.0 %all-gather.4.cloned.1.call-start = ((), (), s32[]{:S(2)}) async-start(), calls=%async_computation.4 | async-start | bytes 4456448 | tf_op jit(solution)/shard_map/all_gather | solution.py:58
  10.5 275.0 %reduce-scatter.9.cloned.1.call-start = ((), (), s32[]{:S(2)}) async-start(), calls=%async_computation.9 | async-start | bytes 4456448 | tf_op jit(solution)/shard_map/reduce_scatter | solution.py:98
  11.7 12.5 %collective-permute-start = (bf16[128,1024]{0,1:T(8,128)(2,1)S(1)}, bf16[128,1024]{0,1:T(8,128)(2,1)S(1)}, u32[]{:S(2)}, u32[]{:S(2)}) collective-permute-start(bf16[128,1024]{0,1:T(8,128)(2,1)S(1)} %copy.66), channel_id=1, source_target_pairs={{0,1},{1,2},{2,3},{3,4},{4,5},{5,6},{6,7},{7,0},{8,9},{9,10},{10,1... | collective-permute-start | bytes 786440 | tf_op jit(solution)/shard_map/ppermute | solution.py:69
  24.2 9.8 %collective-permute-start.1 = (bf16[128,1024]{0,1:T(8,128)(2,1)S(1)}, bf16[128,1024]{0,1:T(8,128)(2,1)S(1)}, u32[]{:S(2)}, u32[]{:S(2)}) collective-permute-start(bf16[128,1024]{0,1:T(8,128)(2,1)S(1)} %collective-permute-done), channel_id=1, source_target_pairs={{0,1},{1,2},{2,3},{3,4},{4,5},{5,6},{6,7},{7,0},{8,9},{9,10},{10,1... | collective-permute-start | bytes 786440 | tf_op jit(solution)/shard_map/ppermute | solution.py:69
  34.0 12.9 %collective-permute-start.2 = (bf16[128,1024]{0,1:T(8,128)(2,1)S(1)}, bf16[128,1024]{0,1:T(8,128)(2,1)S(1)}, u32[]{:S(2)}, u32[]{:S(2)}) collective-permute-start(bf16[128,1024]{0,1:T(8,128)(2,1)S(1)} %collective-permute-done.1), channel_id=1, source_target_pairs={{0,1},{1,2},{2,3},{3,4},{4,5},{5,6},{6,7},{7,0},{8,9},{9,10},{10,1... | collective-permute-start | bytes 786440 | tf_op jit(solution)/shard_map/ppermute | solution.py:69
  46.9 13.2 %collective-permute-start.3 = (bf16[128,1024]{0,1:T(8,128)(2,1)S(1)}, bf16[128,1024]{0,1:T(8,128)(2,1)S(1)}, u32[]{:S(2)}, u32[]{:S(2)}) collective-permute-start(bf16[128,1024]{0,1:T(8,128)(2,1)S(1)} %collective-permute-done.2), channel_id=1, source_target_pairs={{0,1},{1,2},{2,3},{3,4},{4,5},{5,6},{6,7},{7,0},{8,9},{9,10},{10,1... | collective-permute-start | bytes 786440 | tf_op jit(solution)/shard_map/ppermute | solution.py:69
  60.2 7.0 %collective-permute-start.4 = (bf16[128,1024]{0,1:T(8,128)(2,1)S(1)}, bf16[128,1024]{0,1:T(8,128)(2,1)S(1)}, u32[]{:S(2)}, u32[]{:S(2)}) collective-permute-start(bf16[128,1024]{0,1:T(8,128)(2,1)S(1)} %collective-permute-done.3), channel_id=1, source_target_pairs={{0,1},{1,2},{2,3},{3,4},{4,5},{5,6},{6,7},{7,0},{8,9},{9,10},{10,1... | collective-permute-start | bytes 786440 | tf_op jit(solution)/shard_map/ppermute | solution.py:69
  67.2 8.1 %collective-permute-start.5 = (bf16[128,1024]{0,1:T(8,128)(2,1)S(1)}, bf16[128,1024]{0,1:T(8,128)(2,1)S(1)}, u32[]{:S(2)}, u32[]{:S(2)}) collective-permute-start(bf16[128,1024]{0,1:T(8,128)(2,1)S(1)} %collective-permute-done.4), channel_id=1, source_target_pairs={{0,1},{1,2},{2,3},{3,4},{4,5},{5,6},{6,7},{7,0},{8,9},{9,10},{10,1... | collective-permute-start | bytes 786440 | tf_op jit(solution)/shard_map/ppermute | solution.py:69
  75.2 9.4 %collective-permute-start.6 = (bf16[128,1024]{0,1:T(8,128)(2,1)S(1)}, bf16[128,1024]{0,1:T(8,128)(2,1)S(1)}, u32[]{:S(2)}, u32[]{:S(2)}) collective-permute-start(bf16[128,1024]{0,1:T(8,128)(2,1)S(1)} %collective-permute-done.5), channel_id=1, source_target_pairs={{0,1},{1,2},{2,3},{3,4},{4,5},{5,6},{6,7},{7,0},{8,9},{9,10},{10,1... | collective-permute-start | bytes 786440 | tf_op jit(solution)/shard_map/ppermute | solution.py:69
  153.1 5.0 %copy-start.2 = (bf16[128,128,128]{2,1,0:T(8,128)(2,1)S(1)}, bf16[128,128,128]{2,1,0:T(8,128)(2,1)}, u32[]{:S(2)}) copy-start(bf16[128,128,128]{2,1,0:T(8,128)(2,1)} %gather_fusion.4) | copy-start | bytes 12582916
  166.6 137.9 %reduce-scatter.11.cloned.1.call-start = ((), (), s32[]{:S(2)}) async-start(), calls=%async_computation.10 | async-start | bytes 4456448 | tf_op jit(solution)/shard_map/reduce_scatter | solution.py:101
  183.9 162.5 %reduce-scatter.7.cloned.1.call-start = ((), (), s32[]{:S(2)}) async-start(), calls=%async_computation.8 | async-start | bytes 2359296 | tf_op jit(solution)/shard_map/reduce_scatter | solution.py:84
  234.7 155.4 %reduce-scatter.5.cloned.1.call-start = ((), (), s32[]{:S(2)}) async-start(), calls=%async_computation.7 | async-start | bytes 2359296 | tf_op jit(solution)/shard_map/reduce_scatter | solution.py:64
  279.9 161.3 %copy-start.1 = (s32[128,1]{0,1:T(1,128)S(1)}, s32[128,1]{0,1:T(1,128)}, u32[]{:S(2)}) copy-start(s32[128,1]{0,1:T(1,128)} %param.15) | copy-start | bytes 1540
  285.5 152.2 %all-reduce.3.cloned.1.call-start = ((), (), s32[]{:S(2)}) async-start(), calls=%async_computation.11 | async-start | bytes 1048576 | tf_op jit(solution)/shard_map/psum | solution.py:106
Sparse Core Ops, SparseCore 0:
  10.4 52.7 all-gather.7
  65.1 40.8 all-gather.5
  107.8 39.9 all-gather.3
  166.7 66.5 reduce-scatter.8
  235.8 68.6 reduce-scatter.10
  306.9 39.4 reduce-scatter.6
  349.0 41.0 reduce-scatter.4
  392.7 44.9 all-reduce.2
